TPU v7x, 256 devices: a whole 4x4x8 slice. The times are simulated.
256 devices in a mesh: dp: 16 (over z, x_hi), pipe: 4 (over y), tensor: 4 (over x_lo, core).
Axes of the slice: x: 4 (x_hi: 2, x_lo: 2; x = x_hi * 2 + x_lo), y: 4, z: 8, core: 2. Of those that a mesh axis runs over, the one named last changes fastest.
Arguments:
- grad_out: bfloat16 [8, 1024, 4096], P(None, 'dp', 'tensor'), may hold values from -6 to 6
- activations: bfloat16 [4, 3, 8, 1024, 4096], P('pipe', None, None, 'dp', 'tensor'), may hold values from -6 to 6
- mixing: bfloat16 [4, 3, 32, 128, 128], P('pipe', None, 'tensor'), may hold values from -0.1875 to 0.1875
- proj_tiles: bfloat16 [4, 3, 8, 128, 128], P('pipe'), may hold values from -0.1875 to 0.1875
- proj_blocks: int32 [4, 3, 8], P('pipe'), may hold values from 0 to 31, all different within a row
- section_sizes: int32 [4], replicated, may hold values from 1 to 3, 8 in all
Outputs:
- segment_grads: bfloat16 [4, 8, 1024, 4096], P('pipe', None, 'dp', 'tensor')
- sketches: float32 [4, 3, 8, 4096], P('pipe')
Inputs may be any that keep to these rules, and one draw needn't show every extreme that they name: `section_sizes`: each segment holds 1 to 3 layers, 8 in all, some segment exactly 3. `proj_blocks`: the 8 blocks of one slot are distinct.
All inputs are finite; a program needn't handle non-finite values.
Results may differ from a plain program's by a relative error of at most 0.0074.
Values may be sent and summed in bfloat16 or wider, within the bound.
A program may use at most 64 MiB of HBM per device.

v0:
```python
import math
import jax
import jax.numpy as jnp
from jax import lax
from jax.sharding import PartitionSpec as P


def shifted(x, axis, by):
    peers = lax.axis_size(axis)
    pairs = [(i, i + by) for i in range(peers) if 0 <= i + by < peers]
    return lax.ppermute(x, axis, pairs)


def silu_slope(value):
    sig = jax.nn.sigmoid(value)
    return sig * (1.0 + value * (1.0 - sig))


def shards(grad_out, activations, mixing, proj_tiles, proj_blocks, section_sizes):
    high = lax.Precision.HIGHEST
    segments = lax.axis_size("pipe")
    segment = lax.axis_index("pipe")
    half = lax.axis_index("tensor")
    micro = grad_out.shape[0]
    tokens = grad_out.shape[1]
    local_width = grad_out.shape[2]
    slots = activations.shape[1]
    heads_local = mixing.shape[2]
    head_size = mixing.shape[3]
    rank = proj_tiles.shape[4] // 2
    scale = 1.0 / math.sqrt(tokens * lax.axis_size("dp"))
    live_count = section_sizes[segment]
    owned = heads_local * half + jnp.arange(heads_local, dtype=jnp.int32)
    select = (proj_blocks[0][:, :, None] == owned[None, None, :]).astype(jnp.bfloat16)
    dense = jnp.einsum("kjb,kjcr->kbcr", select, proj_tiles[0], preferred_element_type=jnp.float32)
    dense = dense.astype(jnp.bfloat16).reshape(slots, heads_local * head_size, 2 * rank)
    live_slots = jnp.arange(slots, dtype=jnp.int32) < live_count

    def process(grad, start, width):
        acts = lax.dynamic_slice_in_dim(activations[0], start, width, 1)
        act_parts = [None] * slots
        delta_parts = [None] * slots
        for slot in range(slots - 1, -1, -1):
            flat_act = acts[slot].reshape(width * tokens, local_width)
            heads_in = acts[slot].reshape(width, tokens, heads_local, head_size)
            pre = jnp.einsum(
                "mthc,hcd->mthd", heads_in, mixing[0, slot], preferred_element_type=jnp.float32
            )
            grad_heads = grad.reshape(width, tokens, heads_local, head_size).astype(jnp.float32)
            delta = (grad_heads * silu_slope(pre)).astype(jnp.bfloat16)
            back = jnp.einsum(
                "mthd,hcd->mthc", delta, mixing[0, slot], preferred_element_type=jnp.float32
            )
            moved = (grad_heads + back).reshape(width, tokens, local_width).astype(jnp.bfloat16)
            grad = jnp.where(slot < live_count, moved, grad)
            act_parts[slot] = jnp.dot(
                flat_act, dense[slot, :, :rank], preferred_element_type=jnp.float32
            )
            delta_parts[slot] = jnp.dot(
                delta.reshape(width * tokens, local_width),
                dense[slot, :, rank:],
                preferred_element_type=jnp.float32,
            )
        act_proj, grad_proj = lax.psum((jnp.stack(act_parts), jnp.stack(delta_parts)), "tensor")
        act_proj = act_proj.reshape(slots, width, tokens, rank)
        grad_proj = grad_proj.reshape(slots, width, tokens, rank)
        sketch = jnp.einsum("kmtr,kmts->kmrs", grad_proj, act_proj, precision=high) * scale
        sketch = jnp.where(live_slots[:, None, None, None], sketch, 0.0).reshape(
            slots, width, rank * rank
        )
        return (grad, sketch)

    width = 1
    groups = micro // width
    turns = groups + segments - 1

    def turn(step, carry):
        incoming, segment_out, sketches = carry
        group = step - (segments - 1 - segment)
        valid = jnp.logical_and(group >= 0, group < groups)
        start = jnp.clip(group, 0, groups - 1) * width
        top = lax.dynamic_slice_in_dim(grad_out, start, width, 0)
        grad = jnp.where(segment == segments - 1, top, incoming)
        grad, sketch = process(grad, start, width)
        sketch = lax.psum(sketch, "dp")
        old_out = lax.dynamic_slice_in_dim(segment_out, start, width, 0)
        segment_out = lax.dynamic_update_slice_in_dim(
            segment_out, jnp.where(valid, grad, old_out), start, 0
        )
        old_sketch = lax.dynamic_slice_in_dim(sketches, start, width, 1)
        sketches = lax.dynamic_update_slice_in_dim(
            sketches, jnp.where(valid, sketch, old_sketch), start, 1
        )
        incoming = shifted(grad, "pipe", -1)
        return (incoming, segment_out, sketches)

    start_carry = (
        jnp.zeros((width, tokens, local_width), jnp.bfloat16),
        jnp.zeros_like(grad_out),
        jnp.zeros((slots, micro, rank * rank), jnp.float32),
    )
    incoming, segment_out, sketches = lax.fori_loop(0, turns, turn, start_carry)
    return (segment_out[None], sketches[None])


def solution(mesh):
    return jax.shard_map(
        shards,
        mesh=mesh,
        in_specs=(
            P(None, "dp", "tensor"),
            P("pipe", None, None, "dp", "tensor"),
            P("pipe", None, "tensor", None, None),
            P("pipe", None, None, None, None),
            P("pipe", None, None),
            P(),
        ),
        out_specs=(P("pipe", None, "dp", "tensor"), P("pipe", None, None, None)),
        check_vma=False,
    )
```

profile of v0, /device:TPU:8, one launch (start us, length us, event | category | flops | bytes accessed | tf_op | source)
XLA Modules:
  0.0 1463.1 jit_solution(14424018004752751403)
XLA Ops:
  13.3 1442.5 %while.20 = (s32[]{:T(128)}, bf16[1,64,1024]{2,1,0:T(8,128)(2,1)S(1)}, bf16[8,64,1024]{2,1,0:T(8,128)(2,1)}, f32[3,8,4096]{2,1,0:T(8,128)S(1)}, pred[]{:T(512)},...) while((s32[]{:T(128)}, ...), condition=%wide.region_4.5_spmd.clone, body=%wide.region_0.4_spmd.clone.sunk | while | flops 163307520 | bytes 16024470 | solution.py:102
  19.0 4.1 collective-permute-start
  29.5 41.9 %all-reduce.5.cloned.1.call-done = (f32[3,64,64]{2,1,0:T(8,128)}, f32[3,64,64]{2,1,0:T(8,128)}) async-done(((f32[3,64,64]{2,1,0:T(8,128)}, f32[3,64,64]{2,1,0:T(8,128)}), (f32[3,64,64]{2,1,0:T(8,128)}, f32[3,64,64]{2,1,0:T(8,128)})) %all-reduce.5.cloned.1.call-update) | async-done | bytes 98320 | tf_op jit(solution)/shard_map/while/body/eval_jaxpr/psum | solution.py:64
  72.8 77.3 %psum.43 = f32[3,1,4096]{2,0,1:T(4,128)S(1)} all-reduce(f32[3,1,4096]{2,0,1:T(4,128)S(1)} %reshape.292), channel_id=1, replica_groups=mesh['dp'=16,'pipe'=4,'tensor'=4] {'dp'}, use_global_device_ids=true, to_apply=%region_3.3 | all-reduce | flops 12288 | bytes 98304 | tf_op jit(solution)/shard_map/while/body/eval_jaxpr/psum | solution.py:85
  156.3 2.4 collective-permute-start
  165.2 36.7 %all-reduce.5.cloned.1.call-done = (f32[3,64,64]{2,1,0:T(8,128)}, f32[3,64,64]{2,1,0:T(8,128)}) async-done(((f32[3,64,64]{2,1,0:T(8,128)}, f32[3,64,64]{2,1,0:T(8,128)}), (f32[3,64,64]{2,1,0:T(8,128)}, f32[3,64,64]{2,1,0:T(8,128)})) %all-reduce.5.cloned.1.call-update) | async-done | bytes 98320 | tf_op jit(solution)/shard_map/while/body/eval_jaxpr/psum | solution.py:64
  203.3 77.3 %psum.43 = f32[3,1,4096]{2,0,1:T(4,128)S(1)} all-reduce(f32[3,1,4096]{2,0,1:T(4,128)S(1)} %reshape.292), channel_id=1, replica_groups=mesh['dp'=16,'pipe'=4,'tensor'=4] {'dp'}, use_global_device_ids=true, to_apply=%region_3.3 | all-reduce | flops 12288 | bytes 98304 | tf_op jit(solution)/shard_map/while/body/eval_jaxpr/psum | solution.py:85
  286.8 2.4 collective-permute-start
  295.7 36.7 %all-reduce.5.cloned.1.call-done = (f32[3,64,64]{2,1,0:T(8,128)}, f32[3,64,64]{2,1,0:T(8,128)}) async-done(((f32[3,64,64]{2,1,0:T(8,128)}, f32[3,64,64]{2,1,0:T(8,128)}), (f32[3,64,64]{2,1,0:T(8,128)}, f32[3,64,64]{2,1,0:T(8,128)})) %all-reduce.5.cloned.1.call-update) | async-done | bytes 98320 | tf_op jit(solution)/shard_map/while/body/eval_jaxpr/psum | solution.py:64
  333.8 77.3 %psum.43 = f32[3,1,4096]{2,0,1:T(4,128)S(1)} all-reduce(f32[3,1,4096]{2,0,1:T(4,128)S(1)} %reshape.292), channel_id=1, replica_groups=mesh['dp'=16,'pipe'=4,'tensor'=4] {'dp'}, use_global_device_ids=true, to_apply=%region_3.3 | all-reduce | flops 12288 | bytes 98304 | tf_op jit(solution)/shard_map/while/body/eval_jaxpr/psum | solution.py:85
  417.3 2.4 collective-permute-start
  426.2 36.7 %all-reduce.5.cloned.1.call-done = (f32[3,64,64]{2,1,0:T(8,128)}, f32[3,64,64]{2,1,0:T(8,128)}) async-done(((f32[3,64,64]{2,1,0:T(8,128)}, f32[3,64,64]{2,1,0:T(8,128)}), (f32[3,64,64]{2,1,0:T(8,128)}, f32[3,64,64]{2,1,0:T(8,128)})) %all-reduce.5.cloned.1.call-update) | async-done | bytes 98320 | tf_op jit(solution)/shard_map/while/body/eval_jaxpr/psum | solution.py:64
  464.3 77.3 %psum.43 = f32[3,1,4096]{2,0,1:T(4,128)S(1)} all-reduce(f32[3,1,4096]{2,0,1:T(4,128)S(1)} %reshape.292), channel_id=1, replica_groups=mesh['dp'=16,'pipe'=4,'tensor'=4] {'dp'}, use_global_device_ids=true, to_apply=%region_3.3 | all-reduce | flops 12288 | bytes 98304 | tf_op jit(solution)/shard_map/while/body/eval_jaxpr/psum | solution.py:85
  547.8 2.4 collective-permute-start
  556.8 36.7 %all-reduce.5.cloned.1.call-done = (f32[3,64,64]{2,1,0:T(8,128)}, f32[3,64,64]{2,1,0:T(8,128)}) async-done(((f32[3,64,64]{2,1,0:T(8,128)}, f32[3,64,64]{2,1,0:T(8,128)}), (f32[3,64,64]{2,1,0:T(8,128)}, f32[3,64,64]{2,1,0:T(8,128)})) %all-reduce.5.cloned.1.call-update) | async-done | bytes 98320 | tf_op jit(solution)/shard_map/while/body/eval_jaxpr/psum | solution.py:64
  594.9 77.3 %psum.43 = f32[3,1,4096]{2,0,1:T(4,128)S(1)} all-reduce(f32[3,1,4096]{2,0,1:T(4,128)S(1)} %reshape.292), channel_id=1, replica_groups=mesh['dp'=16,'pipe'=4,'tensor'=4] {'dp'}, use_global_device_ids=true, to_apply=%region_3.3 | all-reduce | flops 12288 | bytes 98304 | tf_op jit(solution)/shard_map/while/body/eval_jaxpr/psum | solution.py:85
  687.3 36.7 %all-reduce.5.cloned.1.call-done = (f32[3,64,64]{2,1,0:T(8,128)}, f32[3,64,64]{2,1,0:T(8,128)}) async-done(((f32[3,64,64]{2,1,0:T(8,128)}, f32[3,64,64]{2,1,0:T(8,128)}), (f32[3,64,64]{2,1,0:T(8,128)}, f32[3,64,64]{2,1,0:T(8,128)})) %all-reduce.5.cloned.1.call-update) | async-done | bytes 98320 | tf_op jit(solution)/shard_map/while/body/eval_jaxpr/psum | solution.py:64
  725.4 77.3 %psum.43 = f32[3,1,4096]{2,0,1:T(4,128)S(1)} all-reduce(f32[3,1,4096]{2,0,1:T(4,128)S(1)} %reshape.292), channel_id=1, replica_groups=mesh['dp'=16,'pipe'=4,'tensor'=4] {'dp'}, use_global_device_ids=true, to_apply=%region_3.3 | all-reduce | flops 12288 | bytes 98304 | tf_op jit(solution)/shard_map/while/body/eval_jaxpr/psum | solution.py:85
  808.9 2.4 collective-permute-start
  817.8 36.7 %all-reduce.5.cloned.1.call-done = (f32[3,64,64]{2,1,0:T(8,128)}, f32[3,64,64]{2,1,0:T(8,128)}) async-done(((f32[3,64,64]{2,1,0:T(8,128)}, f32[3,64,64]{2,1,0:T(8,128)}), (f32[3,64,64]{2,1,0:T(8,128)}, f32[3,64,64]{2,1,0:T(8,128)})) %all-reduce.5.cloned.1.call-update) | async-done | bytes 98320 | tf_op jit(solution)/shard_map/while/body/eval_jaxpr/psum | solution.py:64
  855.9 77.3 %psum.43 = f32[3,1,4096]{2,0,1:T(4,128)S(1)} all-reduce(f32[3,1,4096]{2,0,1:T(4,128)S(1)} %reshape.292), channel_id=1, replica_groups=mesh['dp'=16,'pipe'=4,'tensor'=4] {'dp'}, use_global_device_ids=true, to_apply=%region_3.3 | all-reduce | flops 12288 | bytes 98304 | tf_op jit(solution)/shard_map/while/body/eval_jaxpr/psum | solution.py:85
  939.4 2.4 collective-permute-start
  948.3 36.7 %all-reduce.5.cloned.1.call-done = (f32[3,64,64]{2,1,0:T(8,128)}, f32[3,64,64]{2,1,0:T(8,128)}) async-done(((f32[3,64,64]{2,1,0:T(8,128)}, f32[3,64,64]{2,1,0:T(8,128)}), (f32[3,64,64]{2,1,0:T(8,128)}, f32[3,64,64]{2,1,0:T(8,128)})) %all-reduce.5.cloned.1.call-update) | async-done | bytes 98320 | tf_op jit(solution)/shard_map/while/body/eval_jaxpr/psum | solution.py:64
  986.4 77.3 %psum.43 = f32[3,1,4096]{2,0,1:T(4,128)S(1)} all-reduce(f32[3,1,4096]{2,0,1:T(4,128)S(1)} %reshape.292), channel_id=1, replica_groups=mesh['dp'=16,'pipe'=4,'tensor'=4] {'dp'}, use_global_device_ids=true, to_apply=%region_3.3 | all-reduce | flops 12288 | bytes 98304 | tf_op jit(solution)/shard_map/while/body/eval_jaxpr/psum | solution.py:85
  1069.9 2.4 collective-permute-start
  1078.9 36.7 %all-reduce.5.cloned.1.call-done = (f32[3,64,64]{2,1,0:T(8,128)}, f32[3,64,64]{2,1,0:T(8,128)}) async-done(((f32[3,64,64]{2,1,0:T(8,128)}, f32[3,64,64]{2,1,0:T(8,128)}), (f32[3,64,64]{2,1,0:T(8,128)}, f32[3,64,64]{2,1,0:T(8,128)})) %all-reduce.5.cloned.1.call-update) | async-done | bytes 98320 | tf_op jit(solution)/shard_map/while/body/eval_jaxpr/psum | solution.py:64
  1117.0 77.3 %psum.43 = f32[3,1,4096]{2,0,1:T(4,128)S(1)} all-reduce(f32[3,1,4096]{2,0,1:T(4,128)S(1)} %reshape.292), channel_id=1, replica_groups=mesh['dp'=16,'pipe'=4,'tensor'=4] {'dp'}, use_global_device_ids=true, to_apply=%region_3.3 | all-reduce | flops 12288 | bytes 98304 | tf_op jit(solution)/shard_map/while/body/eval_jaxpr/psum | solution.py:85
  1209.4 36.7 %all-reduce.5.cloned.1.call-done = (f32[3,64,64]{2,1,0:T(8,128)}, f32[3,64,64]{2,1,0:T(8,128)}) async-done(((f32[3,64,64]{2,1,0:T(8,128)}, f32[3,64,64]{2,1,0:T(8,128)}), (f32[3,64,64]{2,1,0:T(8,128)}, f32[3,64,64]{2,1,0:T(8,128)})) %all-reduce.5.cloned.1.call-update) | async-done | bytes 98320 | tf_op jit(solution)/shard_map/while/body/eval_jaxpr/psum | solution.py:64
  1247.5 77.3 %psum.43 = f32[3,1,4096]{2,0,1:T(4,128)S(1)} all-reduce(f32[3,1,4096]{2,0,1:T(4,128)S(1)} %reshape.292), channel_id=1, replica_groups=mesh['dp'=16,'pipe'=4,'tensor'=4] {'dp'}, use_global_device_ids=true, to_apply=%region_3.3 | all-reduce | flops 12288 | bytes 98304 | tf_op jit(solution)/shard_map/while/body/eval_jaxpr/psum | solution.py:85
  1331.0 2.4 collective-permute-start
  1339.9 36.7 %all-reduce.5.cloned.1.call-done = (f32[3,64,64]{2,1,0:T(8,128)}, f32[3,64,64]{2,1,0:T(8,128)}) async-done(((f32[3,64,64]{2,1,0:T(8,128)}, f32[3,64,64]{2,1,0:T(8,128)}), (f32[3,64,64]{2,1,0:T(8,128)}, f32[3,64,64]{2,1,0:T(8,128)})) %all-reduce.5.cloned.1.call-update) | async-done | bytes 98320 | tf_op jit(solution)/shard_map/while/body/eval_jaxpr/psum | solution.py:64
  1378.0 77.3 %psum.43 = f32[3,1,4096]{2,0,1:T(4,128)S(1)} all-reduce(f32[3,1,4096]{2,0,1:T(4,128)S(1)} %reshape.292), channel_id=1, replica_groups=mesh['dp'=16,'pipe'=4,'tensor'=4] {'dp'}, use_global_device_ids=true, to_apply=%region_3.3 | all-reduce | flops 12288 | bytes 98304 | tf_op jit(solution)/shard_map/while/body/eval_jaxpr/psum | solution.py:85
  (434 shorter events, 162.2 us)
Async XLA Ops:
  7.2 3.6 copy-start
  7.2 6.1 copy-start.1
  13.3 58.0 %all-reduce.5.cloned.1.call-start = ((), (), s32[]{:S(2)}) async-start(), calls=%async_computation | async-start | bytes 393216 | tf_op jit(solution)/shard_map/while/body/eval_jaxpr/psum | solution.py:64
  19.0 131.6 %collective-permute-start = (bf16[1,64,1024]{2,1,0:T(8,128)(2,1)S(1)}, bf16[1,64,1024]{2,1,0:T(8,128)(2,1)S(1)}, u32[]{:S(2)}, u32[]{:S(2)}) collective-permute-start(bf16[1,64,1024]{2,1,0:T(8,128)(2,1)S(1)} %get-tuple-element.449), channel_id=1, source_target_pairs={{4,0},{8,4},{12,8},{5,1},{9,5},{13,9},{6,2},{10,6},{14,10},{7,3},{... | collective-permute-start | bytes 393224 | tf_op jit(solution)/shard_map/while/body/eval_jaxpr/ppermute | solution.py:11
  150.6 51.3 %all-reduce.5.cloned.1.call-start = ((), (), s32[]{:S(2)}) async-start(), calls=%async_computation | async-start | bytes 393216 | tf_op jit(solution)/shard_map/while/body/eval_jaxpr/psum | solution.py:64
  156.3 124.8 %collective-permute-start = (bf16[1,64,1024]{2,1,0:T(8,128)(2,1)S(1)}, bf16[1,64,1024]{2,1,0:T(8,128)(2,1)S(1)}, u32[]{:S(2)}, u32[]{:S(2)}) collective-permute-start(bf16[1,64,1024]{2,1,0:T(8,128)(2,1)S(1)} %get-tuple-element.449), channel_id=1, source_target_pairs={{4,0},{8,4},{12,8},{5,1},{9,5},{13,9},{6,2},{10,6},{14,10},{7,3},{... | collective-permute-start | bytes 393224 | tf_op jit(solution)/shard_map/while/body/eval_jaxpr/ppermute | solution.py:11
  281.1 51.3 %all-reduce.5.cloned.1.call-start = ((), (), s32[]{:S(2)}) async-start(), calls=%async_computation | async-start | bytes 393216 | tf_op jit(solution)/shard_map/while/body/eval_jaxpr/psum | solution.py:64
  286.8 124.8 %collective-permute-start = (bf16[1,64,1024]{2,1,0:T(8,128)(2,1)S(1)}, bf16[1,64,1024]{2,1,0:T(8,128)(2,1)S(1)}, u32[]{:S(2)}, u32[]{:S(2)}) collective-permute-start(bf16[1,64,1024]{2,1,0:T(8,128)(2,1)S(1)} %get-tuple-element.449), channel_id=1, source_target_pairs={{4,0},{8,4},{12,8},{5,1},{9,5},{13,9},{6,2},{10,6},{14,10},{7,3},{... | collective-permute-start | bytes 393224 | tf_op jit(solution)/shard_map/while/body/eval_jaxpr/ppermute | solution.py:11
  411.6 51.3 %all-reduce.5.cloned.1.call-start = ((), (), s32[]{:S(2)}) async-start(), calls=%async_computation | async-start | bytes 393216 | tf_op jit(solution)/shard_map/while/body/eval_jaxpr/psum | solution.py:64
  417.3 124.8 %collective-permute-start = (bf16[1,64,1024]{2,1,0:T(8,128)(2,1)S(1)}, bf16[1,64,1024]{2,1,0:T(8,128)(2,1)S(1)}, u32[]{:S(2)}, u32[]{:S(2)}) collective-permute-start(bf16[1,64,1024]{2,1,0:T(8,128)(2,1)S(1)} %get-tuple-element.449), channel_id=1, source_target_pairs={{4,0},{8,4},{12,8},{5,1},{9,5},{13,9},{6,2},{10,6},{14,10},{7,3},{... | collective-permute-start | bytes 393224 | tf_op jit(solution)/shard_map/while/body/eval_jaxpr/ppermute | solution.py:11
  542.1 51.3 %all-reduce.5.cloned.1.call-start = ((), (), s32[]{:S(2)}) async-start(), calls=%async_computation | async-start | bytes 393216 | tf_op jit(solution)/shard_map/while/body/eval_jaxpr/psum | solution.py:64
  547.8 124.8 %collective-permute-start = (bf16[1,64,1024]{2,1,0:T(8,128)(2,1)S(1)}, bf16[1,64,1024]{2,1,0:T(8,128)(2,1)S(1)}, u32[]{:S(2)}, u32[]{:S(2)}) collective-permute-start(bf16[1,64,1024]{2,1,0:T(8,128)(2,1)S(1)} %get-tuple-element.449), channel_id=1, source_target_pairs={{4,0},{8,4},{12,8},{5,1},{9,5},{13,9},{6,2},{10,6},{14,10},{7,3},{... | collective-permute-start | bytes 393224 | tf_op jit(solution)/shard_map/while/body/eval_jaxpr/ppermute | solution.py:11
  672.7 51.3 %all-reduce.5.cloned.1.call-start = ((), (), s32[]{:S(2)}) async-start(), calls=%async_computation | async-start | bytes 393216 | tf_op jit(solution)/shard_map/while/body/eval_jaxpr/psum | solution.py:64
  678.4 124.8 %collective-permute-start = (bf16[1,64,1024]{2,1,0:T(8,128)(2,1)S(1)}, bf16[1,64,1024]{2,1,0:T(8,128)(2,1)S(1)}, u32[]{:S(2)}, u32[]{:S(2)}) collective-permute-start(bf16[1,64,1024]{2,1,0:T(8,128)(2,1)S(1)} %get-tuple-element.449), channel_id=1, source_target_pairs={{4,0},{8,4},{12,8},{5,1},{9,5},{13,9},{6,2},{10,6},{14,10},{7,3},{... | collective-permute-start | bytes 393224 | tf_op jit(solution)/shard_map/while/body/eval_jaxpr/ppermute | solution.py:11
  803.2 51.3 %all-reduce.5.cloned.1.call-start = ((), (), s32[]{:S(2)}) async-start(), calls=%async_computation | async-start | bytes 393216 | tf_op jit(solution)/shard_map/while/body/eval_jaxpr/psum | solution.py:64
  808.9 124.8 %collective-permute-start = (bf16[1,64,1024]{2,1,0:T(8,128)(2,1)S(1)}, bf16[1,64,1024]{2,1,0:T(8,128)(2,1)S(1)}, u32[]{:S(2)}, u32[]{:S(2)}) collective-permute-start(bf16[1,64,1024]{2,1,0:T(8,128)(2,1)S(1)} %get-tuple-element.449), channel_id=1, source_target_pairs={{4,0},{8,4},{12,8},{5,1},{9,5},{13,9},{6,2},{10,6},{14,10},{7,3},{... | collective-permute-start | bytes 393224 | tf_op jit(solution)/shard_map/while/body/eval_jaxpr/ppermute | solution.py:11
  933.7 51.3 %all-reduce.5.cloned.1.call-start = ((), (), s32[]{:S(2)}) async-start(), calls=%async_computation | async-start | bytes 393216 | tf_op jit(solution)/shard_map/while/body/eval_jaxpr/psum | solution.py:64
  939.4 124.8 %collective-permute-start = (bf16[1,64,1024]{2,1,0:T(8,128)(2,1)S(1)}, bf16[1,64,1024]{2,1,0:T(8,128)(2,1)S(1)}, u32[]{:S(2)}, u32[]{:S(2)}) collective-permute-start(bf16[1,64,1024]{2,1,0:T(8,128)(2,1)S(1)} %get-tuple-element.449), channel_id=1, source_target_pairs={{4,0},{8,4},{12,8},{5,1},{9,5},{13,9},{6,2},{10,6},{14,10},{7,3},{... | collective-permute-start | bytes 393224 | tf_op jit(solution)/shard_map/while/body/eval_jaxpr/ppermute | solution.py:11
  1064.2 51.3 %all-reduce.5.cloned.1.call-start = ((), (), s32[]{:S(2)}) async-start(), calls=%async_computation | async-start | bytes 393216 | tf_op jit(solution)/shard_map/while/body/eval_jaxpr/psum | solution.py:64
  1069.9 124.8 %collective-permute-start = (bf16[1,64,1024]{2,1,0:T(8,128)(2,1)S(1)}, bf16[1,64,1024]{2,1,0:T(8,128)(2,1)S(1)}, u32[]{:S(2)}, u32[]{:S(2)}) collective-permute-start(bf16[1,64,1024]{2,1,0:T(8,128)(2,1)S(1)} %get-tuple-element.449), channel_id=1, source_target_pairs={{4,0},{8,4},{12,8},{5,1},{9,5},{13,9},{6,2},{10,6},{14,10},{7,3},{... | collective-permute-start | bytes 393224 | tf_op jit(solution)/shard_map/while/body/eval_jaxpr/ppermute | solution.py:11
  1194.8 51.3 %all-reduce.5.cloned.1.call-start = ((), (), s32[]{:S(2)}) async-start(), calls=%async_computation | async-start | bytes 393216 | tf_op jit(solution)/shard_map/while/body/eval_jaxpr/psum | solution.py:64
  1200.5 124.8 %collective-permute-start = (bf16[1,64,1024]{2,1,0:T(8,128)(2,1)S(1)}, bf16[1,64,1024]{2,1,0:T(8,128)(2,1)S(1)}, u32[]{:S(2)}, u32[]{:S(2)}) collective-permute-start(bf16[1,64,1024]{2,1,0:T(8,128)(2,1)S(1)} %get-tuple-element.449), channel_id=1, source_target_pairs={{4,0},{8,4},{12,8},{5,1},{9,5},{13,9},{6,2},{10,6},{14,10},{7,3},{... | collective-permute-start | bytes 393224 | tf_op jit(solution)/shard_map/while/body/eval_jaxpr/ppermute | solution.py:11
  1325.3 51.3 %all-reduce.5.cloned.1.call-start = ((), (), s32[]{:S(2)}) async-start(), calls=%async_computation | async-start | bytes 393216 | tf_op jit(solution)/shard_map/while/body/eval_jaxpr/psum | solution.py:64
  1331.0 124.8 %collective-permute-start = (bf16[1,64,1024]{2,1,0:T(8,128)(2,1)S(1)}, bf16[1,64,1024]{2,1,0:T(8,128)(2,1)S(1)}, u32[]{:S(2)}, u32[]{:S(2)}) collective-permute-start(bf16[1,64,1024]{2,1,0:T(8,128)(2,1)S(1)} %get-tuple-element.449), channel_id=1, source_target_pairs={{4,0},{8,4},{12,8},{5,1},{9,5},{13,9},{6,2},{10,6},{14,10},{7,3},{... | collective-permute-start | bytes 393224 | tf_op jit(solution)/shard_map/while/body/eval_jaxpr/ppermute | solution.py:11
  1455.8 0.7 copy-start.2
Sparse Core Ops, SparseCore 0:
  28.9 42.4 all-reduce.4
  164.6 37.2 all-reduce.4
  295.1 37.2 all-reduce.4
  425.6 37.2 all-reduce.4
  556.1 37.2 all-reduce.4
  686.7 37.2 all-reduce.4
  817.2 37.2 all-reduce.4
  947.7 37.2 all-reduce.4
  1078.2 37.2 all-reduce.4
  1208.8 37.2 all-reduce.4
  1339.3 37.2 all-reduce.4
where the time goes:
time: 1470 us; the launch traced here: 1460 us
  blocking collectives  850 us (58%)
  waiting for transfers between devices  409 us (28%)
  matrix products  77.6 us (5%)
  other arithmetic  51.4 us (3%)
  starting transfers between devices  28.8 us (2%)
  local copies, waits for them, and re-layouts  27.7 us (2%)
  between operations  15.8 us (1%)
    psum x11, blocking collectives, turn(): sketch = lax.psum(sketch, 'dp')  850 us
    psum x11, waiting for transfers between devices, process(): lax.psum((jnp.stack(act_parts), jnp.stack(delta_parts)), 'tensor')  409 us
    dot_general x33, matrix products, process(): jnp.dot(flat_act, dense[slot, :, :rank], preferred_element_type=jnp.float32)  35.7 us
  transfers between devices with their start and end apart: 22, of which 11 were waited for; matrix products, arithmetic and copies ran while one was open for 6% of the time, Pallas kernels for 0%

commit v1 on v0

--- a/solution.py
+++ b/solution.py
@@ -82,7 +82,7 @@
         top = lax.dynamic_slice_in_dim(grad_out, start, width, 0)
         grad = jnp.where(segment == segments - 1, top, incoming)
         grad, sketch = process(grad, start, width)
-        sketch = lax.psum(sketch, "dp")
+        sketch = jnp.sum(lax.all_gather(sketch, "dp"), axis=0)
         old_out = lax.dynamic_slice_in_dim(segment_out, start, width, 0)
         segment_out = lax.dynamic_update_slice_in_dim(
             segment_out, jnp.where(valid, grad, old_out), start, 0

time: 1470 us -> 1150 us (0.78)
  blocking collectives: 850 us -> 503 us
  other arithmetic: 51.4 us -> 69.6 us
  local copies, waits for them, and re-layouts: 27.7 us -> 42.5 us
    psum x11 -> x0, blocking collectives: 850 us -> none  [turn(): sketch = lax.psum(sketch, 'dp')]
    all_gather x0 -> x11, blocking collectives: none -> 503 us  [turn(): sketch = jnp.sum(lax.all_gather(sketch, 'dp'), axis=0)]
    dynamic_update_slice x22 -> x11, local copies, waits for them, and re-layouts: 4.96 us -> 20.2 us  [turn(): lax.dynamic_update_slice_in_dim(sketches, jnp.where(valid, sketch, old_sk...]
  transfers between devices with their start and end apart: 22 -> 22, of which waited for: 11 -> 11; matrix products, arithmetic and copies ran while one was open for 6% -> 11% of each run, Pallas kernels for 0% -> 0%
where the time goes in v1:
time: 1150 us
  blocking collectives  503 us (44%)
  waiting for transfers between devices  411 us (36%)
  matrix products  77.6 us (7%)
  other arithmetic  69.6 us (6%)
  local copies, waits for them, and re-layouts  42.5 us (4%)
  starting transfers between devices  28.4 us (2%)
  between operations  15.7 us (1%)
    all_gather x11, blocking collectives, turn(): sketch = jnp.sum(lax.all_gather(sketch, 'dp'), axis=0)  503 us
    psum x11, waiting for transfers between devices, process(): lax.psum((jnp.stack(act_parts), jnp.stack(delta_parts)), 'tensor')  411 us
    dot_general x33, matrix products, process(): jnp.dot(flat_act, dense[slot, :, :rank], preferred_element_type=jnp.float32)  35.7 us
    ppermute x11, starting transfers between devices, shifted(): return lax.ppermute(x, axis, pairs)  28.4 us
  transfers between devices with their start and end apart: 22, of which 11 were waited for; matrix products, arithmetic and copies ran while one was open for 11% of the time, Pallas kernels for 0%

profile of v1, /device:TPU:8, one launch (start us, length us, event | category | flops | bytes accessed | tf_op | source)
XLA Modules:
  0.0 1150.0 jit_solution(5238791477257663822)
XLA Ops:
  13.9 1129.6 %while.20 = (s32[]{:T(128)}, bf16[1,64,1024]{2,1,0:T(8,128)(2,1)S(1)}, bf16[8,64,1024]{2,1,0:T(8,128)(2,1)}, f32[3,8,4096]{2,1,0:T(8,128)}, pred[]{:T(512)}, /*i...) while((s32[]{:T(128)}, ...), condition=%wide.region_4.5_spmd.clone, body=%wide.region_0.4_spmd.clone.sunk | while | flops 163479552 | bytes 17400736 | solution.py:102
  19.5 4.1 collective-permute-start
  30.0 42.0 %all-reduce.5.cloned.1.call-done = (f32[3,64,64]{2,1,0:T(8,128)}, f32[3,64,64]{2,1,0:T(8,128)}) async-done(((f32[3,64,64]{2,1,0:T(8,128)}, f32[3,64,64]{2,1,0:T(8,128)}), (f32[3,64,64]{2,1,0:T(8,128)}, f32[3,64,64]{2,1,0:T(8,128)})) %all-reduce.5.cloned.1.call-update) | async-done | bytes 98320 | tf_op jit(solution)/shard_map/while/body/eval_jaxpr/psum | solution.py:64
  73.3 45.7 %all_gather.11 = f32[16,3,1,4096]{3,2,1,0:T(1,128)S(1)} all-gather(f32[1,3,1,4096]{3,2,1,0:T(1,128)S(1)} %reshape.298), channel_id=1, replica_groups=mesh['dp'=16,'pipe'=4,'tensor'=4] {'dp'}, dimensions={0}, use_global_device_ids=true | all-gather | bytes 835584 | tf_op jit(solution)/shard_map/while/body/eval_jaxpr/all_gather | solution.py:85
  128.3 2.4 collective-permute-start
  137.1 36.9 %all-reduce.5.cloned.1.call-done = (f32[3,64,64]{2,1,0:T(8,128)}, f32[3,64,64]{2,1,0:T(8,128)}) async-done(((f32[3,64,64]{2,1,0:T(8,128)}, f32[3,64,64]{2,1,0:T(8,128)}), (f32[3,64,64]{2,1,0:T(8,128)}, f32[3,64,64]{2,1,0:T(8,128)})) %all-reduce.5.cloned.1.call-update) | async-done | bytes 98320 | tf_op jit(solution)/shard_map/while/body/eval_jaxpr/psum | solution.py:64
  175.4 45.7 %all_gather.11 = f32[16,3,1,4096]{3,2,1,0:T(1,128)S(1)} all-gather(f32[1,3,1,4096]{3,2,1,0:T(1,128)S(1)} %reshape.298), channel_id=1, replica_groups=mesh['dp'=16,'pipe'=4,'tensor'=4] {'dp'}, dimensions={0}, use_global_device_ids=true | all-gather | bytes 835584 | tf_op jit(solution)/shard_map/while/body/eval_jaxpr/all_gather | solution.py:85
  230.4 2.4 collective-permute-start
  239.2 36.9 %all-reduce.5.cloned.1.call-done = (f32[3,64,64]{2,1,0:T(8,128)}, f32[3,64,64]{2,1,0:T(8,128)}) async-done(((f32[3,64,64]{2,1,0:T(8,128)}, f32[3,64,64]{2,1,0:T(8,128)}), (f32[3,64,64]{2,1,0:T(8,128)}, f32[3,64,64]{2,1,0:T(8,128)})) %all-reduce.5.cloned.1.call-update) | async-done | bytes 98320 | tf_op jit(solution)/shard_map/while/body/eval_jaxpr/psum | solution.py:64
  277.5 45.7 %all_gather.11 = f32[16,3,1,4096]{3,2,1,0:T(1,128)S(1)} all-gather(f32[1,3,1,4096]{3,2,1,0:T(1,128)S(1)} %reshape.298), channel_id=1, replica_groups=mesh['dp'=16,'pipe'=4,'tensor'=4] {'dp'}, dimensions={0}, use_global_device_ids=true | all-gather | bytes 835584 | tf_op jit(solution)/shard_map/while/body/eval_jaxpr/all_gather | solution.py:85
  332.5 2.4 collective-permute-start
  341.3 36.9 %all-reduce.5.cloned.1.call-done = (f32[3,64,64]{2,1,0:T(8,128)}, f32[3,64,64]{2,1,0:T(8,128)}) async-done(((f32[3,64,64]{2,1,0:T(8,128)}, f32[3,64,64]{2,1,0:T(8,128)}), (f32[3,64,64]{2,1,0:T(8,128)}, f32[3,64,64]{2,1,0:T(8,128)})) %all-reduce.5.cloned.1.call-update) | async-done | bytes 98320 | tf_op jit(solution)/shard_map/while/body/eval_jaxpr/psum | solution.py:64
  379.6 45.7 %all_gather.11 = f32[16,3,1,4096]{3,2,1,0:T(1,128)S(1)} all-gather(f32[1,3,1,4096]{3,2,1,0:T(1,128)S(1)} %reshape.298), channel_id=1, replica_groups=mesh['dp'=16,'pipe'=4,'tensor'=4] {'dp'}, dimensions={0}, use_global_device_ids=true | all-gather | bytes 835584 | tf_op jit(solution)/shard_map/while/body/eval_jaxpr/all_gather | solution.py:85
  434.5 2.4 collective-permute-start
  443.4 36.9 %all-reduce.5.cloned.1.call-done = (f32[3,64,64]{2,1,0:T(8,128)}, f32[3,64,64]{2,1,0:T(8,128)}) async-done(((f32[3,64,64]{2,1,0:T(8,128)}, f32[3,64,64]{2,1,0:T(8,128)}), (f32[3,64,64]{2,1,0:T(8,128)}, f32[3,64,64]{2,1,0:T(8,128)})) %all-reduce.5.cloned.1.call-update) | async-done | bytes 98320 | tf_op jit(solution)/shard_map/while/body/eval_jaxpr/psum | solution.py:64
  481.7 45.7 %all_gather.11 = f32[16,3,1,4096]{3,2,1,0:T(1,128)S(1)} all-gather(f32[1,3,1,4096]{3,2,1,0:T(1,128)S(1)} %reshape.298), channel_id=1, replica_groups=mesh['dp'=16,'pipe'=4,'tensor'=4] {'dp'}, dimensions={0}, use_global_device_ids=true | all-gather | bytes 835584 | tf_op jit(solution)/shard_map/while/body/eval_jaxpr/all_gather | solution.py:85
  545.4 36.9 %all-reduce.5.cloned.1.call-done = (f32[3,64,64]{2,1,0:T(8,128)}, f32[3,64,64]{2,1,0:T(8,128)}) async-done(((f32[3,64,64]{2,1,0:T(8,128)}, f32[3,64,64]{2,1,0:T(8,128)}), (f32[3,64,64]{2,1,0:T(8,128)}, f32[3,64,64]{2,1,0:T(8,128)})) %all-reduce.5.cloned.1.call-update) | async-done | bytes 98320 | tf_op jit(solution)/shard_map/while/body/eval_jaxpr/psum | solution.py:64
  583.7 45.7 %all_gather.11 = f32[16,3,1,4096]{3,2,1,0:T(1,128)S(1)} all-gather(f32[1,3,1,4096]{3,2,1,0:T(1,128)S(1)} %reshape.298), channel_id=1, replica_groups=mesh['dp'=16,'pipe'=4,'tensor'=4] {'dp'}, dimensions={0}, use_global_device_ids=true | all-gather | bytes 835584 | tf_op jit(solution)/shard_map/while/body/eval_jaxpr/all_gather | solution.py:85
  638.7 2.4 collective-permute-start
  647.5 36.9 %all-reduce.5.cloned.1.call-done = (f32[3,64,64]{2,1,0:T(8,128)}, f32[3,64,64]{2,1,0:T(8,128)}) async-done(((f32[3,64,64]{2,1,0:T(8,128)}, f32[3,64,64]{2,1,0:T(8,128)}), (f32[3,64,64]{2,1,0:T(8,128)}, f32[3,64,64]{2,1,0:T(8,128)})) %all-reduce.5.cloned.1.call-update) | async-done | bytes 98320 | tf_op jit(solution)/shard_map/while/body/eval_jaxpr/psum | solution.py:64
  685.8 45.7 %all_gather.11 = f32[16,3,1,4096]{3,2,1,0:T(1,128)S(1)} all-gather(f32[1,3,1,4096]{3,2,1,0:T(1,128)S(1)} %reshape.298), channel_id=1, replica_groups=mesh['dp'=16,'pipe'=4,'tensor'=4] {'dp'}, dimensions={0}, use_global_device_ids=true | all-gather | bytes 835584 | tf_op jit(solution)/shard_map/while/body/eval_jaxpr/all_gather | solution.py:85
  740.8 2.4 collective-permute-start
  749.6 36.9 %all-reduce.5.cloned.1.call-done = (f32[3,64,64]{2,1,0:T(8,128)}, f32[3,64,64]{2,1,0:T(8,128)}) async-done(((f32[3,64,64]{2,1,0:T(8,128)}, f32[3,64,64]{2,1,0:T(8,128)}), (f32[3,64,64]{2,1,0:T(8,128)}, f32[3,64,64]{2,1,0:T(8,128)})) %all-reduce.5.cloned.1.call-update) | async-done | bytes 98320 | tf_op jit(solution)/shard_map/while/body/eval_jaxpr/psum | solution.py:64
  787.9 45.7 %all_gather.11 = f32[16,3,1,4096]{3,2,1,0:T(1,128)S(1)} all-gather(f32[1,3,1,4096]{3,2,1,0:T(1,128)S(1)} %reshape.298), channel_id=1, replica_groups=mesh['dp'=16,'pipe'=4,'tensor'=4] {'dp'}, dimensions={0}, use_global_device_ids=true | all-gather | bytes 835584 | tf_op jit(solution)/shard_map/while/body/eval_jaxpr/all_gather | solution.py:85
  851.7 36.9 %all-reduce.5.cloned.1.call-done = (f32[3,64,64]{2,1,0:T(8,128)}, f32[3,64,64]{2,1,0:T(8,128)}) async-done(((f32[3,64,64]{2,1,0:T(8,128)}, f32[3,64,64]{2,1,0:T(8,128)}), (f32[3,64,64]{2,1,0:T(8,128)}, f32[3,64,64]{2,1,0:T(8,128)})) %all-reduce.5.cloned.1.call-update) | async-done | bytes 98320 | tf_op jit(solution)/shard_map/while/body/eval_jaxpr/psum | solution.py:64
  890.0 45.7 %all_gather.11 = f32[16,3,1,4096]{3,2,1,0:T(1,128)S(1)} all-gather(f32[1,3,1,4096]{3,2,1,0:T(1,128)S(1)} %reshape.298), channel_id=1, replica_groups=mesh['dp'=16,'pipe'=4,'tensor'=4] {'dp'}, dimensions={0}, use_global_device_ids=true | all-gather | bytes 835584 | tf_op jit(solution)/shard_map/while/body/eval_jaxpr/all_gather | solution.py:85
  944.9 2.4 collective-permute-start
  953.8 36.9 %all-reduce.5.cloned.1.call-done = (f32[3,64,64]{2,1,0:T(8,128)}, f32[3,64,64]{2,1,0:T(8,128)}) async-done(((f32[3,64,64]{2,1,0:T(8,128)}, f32[3,64,64]{2,1,0:T(8,128)}), (f32[3,64,64]{2,1,0:T(8,128)}, f32[3,64,64]{2,1,0:T(8,128)})) %all-reduce.5.cloned.1.call-update) | async-done | bytes 98320 | tf_op jit(solution)/shard_map/while/body/eval_jaxpr/psum | solution.py:64
  992.0 45.7 %all_gather.11 = f32[16,3,1,4096]{3,2,1,0:T(1,128)S(1)} all-gather(f32[1,3,1,4096]{3,2,1,0:T(1,128)S(1)} %reshape.298), channel_id=1, replica_groups=mesh['dp'=16,'pipe'=4,'tensor'=4] {'dp'}, dimensions={0}, use_global_device_ids=true | all-gather | bytes 835584 | tf_op jit(solution)/shard_map/while/body/eval_jaxpr/all_gather | solution.py:85
  1047.0 2.4 collective-permute-start
  1055.8 36.9 %all-reduce.5.cloned.1.call-done = (f32[3,64,64]{2,1,0:T(8,128)}, f32[3,64,64]{2,1,0:T(8,128)}) async-done(((f32[3,64,64]{2,1,0:T(8,128)}, f32[3,64,64]{2,1,0:T(8,128)}), (f32[3,64,64]{2,1,0:T(8,128)}, f32[3,64,64]{2,1,0:T(8,128)})) %all-reduce.5.cloned.1.call-update) | async-done | bytes 98320 | tf_op jit(solution)/shard_map/while/body/eval_jaxpr/psum | solution.py:64
  1094.1 45.7 %all_gather.11 = f32[16,3,1,4096]{3,2,1,0:T(1,128)S(1)} all-gather(f32[1,3,1,4096]{3,2,1,0:T(1,128)S(1)} %reshape.298), channel_id=1, replica_groups=mesh['dp'=16,'pipe'=4,'tensor'=4] {'dp'}, dimensions={0}, use_global_device_ids=true | all-gather | bytes 835584 | tf_op jit(solution)/shard_map/while/body/eval_jaxpr/all_gather | solution.py:85
  (421 shorter events, 194.8 us)
Async XLA Ops:
  7.2 3.4 copy-start
  7.2 6.7 copy-start.1
  13.9 58.0 %all-reduce.5.cloned.1.call-start = ((), (), s32[]{:S(2)}) async-start(), calls=%async_computation | async-start | bytes 393216 | tf_op jit(solution)/shard_map/while/body/eval_jaxpr/psum | solution.py:64
  19.5 103.1 %collective-permute-start = (bf16[1,64,1024]{2,1,0:T(8,128)(2,1)S(1)}, bf16[1,64,1024]{2,1,0:T(8,128)(2,1)S(1)}, u32[]{:S(2)}, u32[]{:S(2)}) collective-permute-start(bf16[1,64,1024]{2,1,0:T(8,128)(2,1)S(1)} %get-tuple-element.449), channel_id=1, source_target_pairs={{4,0},{8,4},{12,8},{5,1},{9,5},{13,9},{6,2},{10,6},{14,10},{7,3},{... | collective-permute-start | bytes 393224 | tf_op jit(solution)/shard_map/while/body/eval_jaxpr/ppermute | solution.py:11
  122.7 51.4 %all-reduce.5.cloned.1.call-start = ((), (), s32[]{:S(2)}) async-start(), calls=%async_computation | async-start | bytes 393216 | tf_op jit(solution)/shard_map/while/body/eval_jaxpr/psum | solution.py:64
  128.3 96.5 %collective-permute-start = (bf16[1,64,1024]{2,1,0:T(8,128)(2,1)S(1)}, bf16[1,64,1024]{2,1,0:T(8,128)(2,1)S(1)}, u32[]{:S(2)}, u32[]{:S(2)}) collective-permute-start(bf16[1,64,1024]{2,1,0:T(8,128)(2,1)S(1)} %get-tuple-element.449), channel_id=1, source_target_pairs={{4,0},{8,4},{12,8},{5,1},{9,5},{13,9},{6,2},{10,6},{14,10},{7,3},{... | collective-permute-start | bytes 393224 | tf_op jit(solution)/shard_map/while/body/eval_jaxpr/ppermute | solution.py:11
  224.8 51.3 %all-reduce.5.cloned.1.call-start = ((), (), s32[]{:S(2)}) async-start(), calls=%async_computation | async-start | bytes 393216 | tf_op jit(solution)/shard_map/while/body/eval_jaxpr/psum | solution.py:64
  230.4 96.4 %collective-permute-start = (bf16[1,64,1024]{2,1,0:T(8,128)(2,1)S(1)}, bf16[1,64,1024]{2,1,0:T(8,128)(2,1)S(1)}, u32[]{:S(2)}, u32[]{:S(2)}) collective-permute-start(bf16[1,64,1024]{2,1,0:T(8,128)(2,1)S(1)} %get-tuple-element.449), channel_id=1, source_target_pairs={{4,0},{8,4},{12,8},{5,1},{9,5},{13,9},{6,2},{10,6},{14,10},{7,3},{... | collective-permute-start | bytes 393224 | tf_op jit(solution)/shard_map/while/body/eval_jaxpr/ppermute | solution.py:11
  326.8 51.3 %all-reduce.5.cloned.1.call-start = ((), (), s32[]{:S(2)}) async-start(), calls=%async_computation | async-start | bytes 393216 | tf_op jit(solution)/shard_map/while/body/eval_jaxpr/psum | solution.py:64
  332.5 96.4 %collective-permute-start = (bf16[1,64,1024]{2,1,0:T(8,128)(2,1)S(1)}, bf16[1,64,1024]{2,1,0:T(8,128)(2,1)S(1)}, u32[]{:S(2)}, u32[]{:S(2)}) collective-permute-start(bf16[1,64,1024]{2,1,0:T(8,128)(2,1)S(1)} %get-tuple-element.449), channel_id=1, source_target_pairs={{4,0},{8,4},{12,8},{5,1},{9,5},{13,9},{6,2},{10,6},{14,10},{7,3},{... | collective-permute-start | bytes 393224 | tf_op jit(solution)/shard_map/while/body/eval_jaxpr/ppermute | solution.py:11
  428.9 51.3 %all-reduce.5.cloned.1.call-start = ((), (), s32[]{:S(2)}) async-start(), calls=%async_computation | async-start | bytes 393216 | tf_op jit(solution)/shard_map/while/body/eval_jaxpr/psum | solution.py:64
  434.5 96.4 %collective-permute-start = (bf16[1,64,1024]{2,1,0:T(8,128)(2,1)S(1)}, bf16[1,64,1024]{2,1,0:T(8,128)(2,1)S(1)}, u32[]{:S(2)}, u32[]{:S(2)}) collective-permute-start(bf16[1,64,1024]{2,1,0:T(8,128)(2,1)S(1)} %get-tuple-element.449), channel_id=1, source_target_pairs={{4,0},{8,4},{12,8},{5,1},{9,5},{13,9},{6,2},{10,6},{14,10},{7,3},{... | collective-permute-start | bytes 393224 | tf_op jit(solution)/shard_map/while/body/eval_jaxpr/ppermute | solution.py:11
  531.0 51.3 %all-reduce.5.cloned.1.call-start = ((), (), s32[]{:S(2)}) async-start(), calls=%async_computation | async-start | bytes 393216 | tf_op jit(solution)/shard_map/while/body/eval_jaxpr/psum | solution.py:64
  536.6 96.4 %collective-permute-start = (bf16[1,64,1024]{2,1,0:T(8,128)(2,1)S(1)}, bf16[1,64,1024]{2,1,0:T(8,128)(2,1)S(1)}, u32[]{:S(2)}, u32[]{:S(2)}) collective-permute-start(bf16[1,64,1024]{2,1,0:T(8,128)(2,1)S(1)} %get-tuple-element.449), channel_id=1, source_target_pairs={{4,0},{8,4},{12,8},{5,1},{9,5},{13,9},{6,2},{10,6},{14,10},{7,3},{... | collective-permute-start | bytes 393224 | tf_op jit(solution)/shard_map/while/body/eval_jaxpr/ppermute | solution.py:11
  633.1 51.3 %all-reduce.5.cloned.1.call-start = ((), (), s32[]{:S(2)}) async-start(), calls=%async_computation | async-start | bytes 393216 | tf_op jit(solution)/shard_map/while/body/eval_jaxpr/psum | solution.py:64
  638.7 96.4 %collective-permute-start = (bf16[1,64,1024]{2,1,0:T(8,128)(2,1)S(1)}, bf16[1,64,1024]{2,1,0:T(8,128)(2,1)S(1)}, u32[]{:S(2)}, u32[]{:S(2)}) collective-permute-start(bf16[1,64,1024]{2,1,0:T(8,128)(2,1)S(1)} %get-tuple-element.449), channel_id=1, source_target_pairs={{4,0},{8,4},{12,8},{5,1},{9,5},{13,9},{6,2},{10,6},{14,10},{7,3},{... | collective-permute-start | bytes 393224 | tf_op jit(solution)/shard_map/while/body/eval_jaxpr/ppermute | solution.py:11
  735.1 51.3 %all-reduce.5.cloned.1.call-start = ((), (), s32[]{:S(2)}) async-start(), calls=%async_computation | async-start | bytes 393216 | tf_op jit(solution)/shard_map/while/body/eval_jaxpr/psum | solution.py:64
  740.8 96.4 %collective-permute-start = (bf16[1,64,1024]{2,1,0:T(8,128)(2,1)S(1)}, bf16[1,64,1024]{2,1,0:T(8,128)(2,1)S(1)}, u32[]{:S(2)}, u32[]{:S(2)}) collective-permute-start(bf16[1,64,1024]{2,1,0:T(8,128)(2,1)S(1)} %get-tuple-element.449), channel_id=1, source_target_pairs={{4,0},{8,4},{12,8},{5,1},{9,5},{13,9},{6,2},{10,6},{14,10},{7,3},{... | collective-permute-start | bytes 393224 | tf_op jit(solution)/shard_map/while/body/eval_jaxpr/ppermute | solution.py:11
  837.2 51.3 %all-reduce.5.cloned.1.call-start = ((), (), s32[]{:S(2)}) async-start(), calls=%async_computation | async-start | bytes 393216 | tf_op jit(solution)/shard_map/while/body/eval_jaxpr/psum | solution.py:64
  842.9 96.4 %collective-permute-start = (bf16[1,64,1024]{2,1,0:T(8,128)(2,1)S(1)}, bf16[1,64,1024]{2,1,0:T(8,128)(2,1)S(1)}, u32[]{:S(2)}, u32[]{:S(2)}) collective-permute-start(bf16[1,64,1024]{2,1,0:T(8,128)(2,1)S(1)} %get-tuple-element.449), channel_id=1, source_target_pairs={{4,0},{8,4},{12,8},{5,1},{9,5},{13,9},{6,2},{10,6},{14,10},{7,3},{... | collective-permute-start | bytes 393224 | tf_op jit(solution)/shard_map/while/body/eval_jaxpr/ppermute | solution.py:11
  939.3 51.3 %all-reduce.5.cloned.1.call-start = ((), (), s32[]{:S(2)}) async-start(), calls=%async_computation | async-start | bytes 393216 | tf_op jit(solution)/shard_map/while/body/eval_jaxpr/psum | solution.py:64
  944.9 96.4 %collective-permute-start = (bf16[1,64,1024]{2,1,0:T(8,128)(2,1)S(1)}, bf16[1,64,1024]{2,1,0:T(8,128)(2,1)S(1)}, u32[]{:S(2)}, u32[]{:S(2)}) collective-permute-start(bf16[1,64,1024]{2,1,0:T(8,128)(2,1)S(1)} %get-tuple-element.449), channel_id=1, source_target_pairs={{4,0},{8,4},{12,8},{5,1},{9,5},{13,9},{6,2},{10,6},{14,10},{7,3},{... | collective-permute-start | bytes 393224 | tf_op jit(solution)/shard_map/while/body/eval_jaxpr/ppermute | solution.py:11
  1041.4 51.3 %all-reduce.5.cloned.1.call-start = ((), (), s32[]{:S(2)}) async-start(), calls=%async_computation | async-start | bytes 393216 | tf_op jit(solution)/shard_map/while/body/eval_jaxpr/psum | solution.py:64
  1047.0 96.4 %collective-permute-start = (bf16[1,64,1024]{2,1,0:T(8,128)(2,1)S(1)}, bf16[1,64,1024]{2,1,0:T(8,128)(2,1)S(1)}, u32[]{:S(2)}, u32[]{:S(2)}) collective-permute-start(bf16[1,64,1024]{2,1,0:T(8,128)(2,1)S(1)} %get-tuple-element.449), channel_id=1, source_target_pairs={{4,0},{8,4},{12,8},{5,1},{9,5},{13,9},{6,2},{10,6},{14,10},{7,3},{... | collective-permute-start | bytes 393224 | tf_op jit(solution)/shard_map/while/body/eval_jaxpr/ppermute | solution.py:11
Sparse Core Ops, SparseCore 0:
  29.5 42.4 all-reduce.4
  136.6 37.3 all-reduce.4
  238.7 37.3 all-reduce.4
  340.8 37.3 all-reduce.4
  442.8 37.3 all-reduce.4
  544.9 37.3 all-reduce.4
  647.0 37.3 all-reduce.4
  749.1 37.3 all-reduce.4
  851.2 37.3 all-reduce.4
  953.2 37.3 all-reduce.4
  1055.3 37.3 all-reduce.4
